TPU v7x, 32 devices: a whole 2x2x4 slice. The times are simulated.
32 devices in a mesh: chain: 2 (over x), slab: 16 (over z, y, core).
Axes of the slice: x: 2, y: 2, z: 4, core: 2. Of those that a mesh axis runs over, the one named last changes fastest.
Arguments:
- whitened: float32 [1024, 256, 256], P(('chain', 'slab')), parts along dimension 0, may hold values from -6 to 6
- counts: int32 [1024, 256, 256], P(('chain', 'slab')), parts along dimension 0, may hold values from 0 to 24
- exposure: int32 [1024, 256, 256], P(('chain', 'slab')), parts along dimension 0, may hold values from 1 to 12
- cholesky_east: float32 [512, 512], replicated, as said below
- cholesky_north: float32 [256, 256], replicated, as said below
- cholesky_time: float32 [256, 256], replicated, as said below
Outputs:
- gradient: float32 [1024, 256, 256], P(('chain', 'slab')), parts along dimension 0
- density: float32 [2], P('chain'), parts along dimension 0
There are 2 independent parts, one for each index of `chain`. A program takes and returns all parts, laid end to end along the dimension named above; an argument that names none is the same for every part. Nothing has to cross between parts.
Inputs may be any that keep to these rules, and one draw needn't show every extreme that they name: `cholesky_east`: lower triangular with a positive diagonal, each row of unit length. `cholesky_north`: lower triangular with a positive diagonal, each row of unit length. `cholesky_time`: lower triangular with a positive diagonal, each row of unit length.
All inputs are finite; a program needn't handle non-finite values.
Results may differ from a plain program's by a relative error of at most 0.00008.
Values sent between devices are 32-bit elements; how exact they have to be, the bound alone decides.
A program may use at most 128 MiB of HBM per device.

v0:
```python
import jax
import jax.numpy as jnp
from jax import lax
from jax.sharding import PartitionSpec as P

field_scale = 0.6


def mode_last(values, matrix):
    return jnp.einsum("abc,tc->abt", values, matrix, precision=lax.Precision.HIGHEST)


def mode_middle(values, matrix):
    return jnp.einsum("abc,yb->ayc", values, matrix, precision=lax.Precision.HIGHEST)


def mode_first(values, matrix):
    return jnp.einsum("abc,xa->xbc", values, matrix, precision=lax.Precision.HIGHEST)


def adjoint_last(values, matrix):
    return jnp.einsum("abt,tc->abc", values, matrix, precision=lax.Precision.HIGHEST)


def adjoint_middle(values, matrix):
    return jnp.einsum("ayc,yb->abc", values, matrix, precision=lax.Precision.HIGHEST)


def adjoint_first(values, matrix):
    return jnp.einsum("xbc,xa->abc", values, matrix, precision=lax.Precision.HIGHEST)


def to_lines(values):
    return lax.all_to_all(values, "slab", split_axis=1, concat_axis=0, tiled=True)


def to_planes(values):
    return lax.all_to_all(values, "slab", split_axis=0, concat_axis=1, tiled=True)


def per_device(whitened, counts, exposure, cholesky_east, cholesky_north, cholesky_time):
    cell_count = whitened.shape[0] * whitened.shape[1] * whitened.shape[2]
    prior_term = -0.5 * jnp.sum(whitened * whitened)
    partly = mode_middle(mode_last(whitened, cholesky_time), cholesky_north)
    counts_lines, exposure_lines = (
        lax.all_to_all(counts, "slab", split_axis=1, concat_axis=0, tiled=True),
        lax.all_to_all(exposure, "slab", split_axis=1, concat_axis=0, tiled=True),
    )
    log_lines = field_scale * mode_first(to_lines(partly), cholesky_east)
    observed = counts_lines.astype(jnp.float32)
    intensity = exposure_lines.astype(jnp.float32) * jnp.exp(log_lines)
    residual = observed - intensity
    partial_sum = jnp.sum(observed * log_lines - intensity) + prior_term
    adjoint_lines = adjoint_first(residual, cholesky_east)
    adjoint = to_planes(adjoint_lines)
    adjoint = adjoint_last(adjoint_middle(adjoint, cholesky_north), cholesky_time)
    gradient = field_scale * adjoint - whitened
    total_sum = lax.psum(partial_sum, "slab")
    density = total_sum / (cell_count * lax.axis_size("slab"))
    return (gradient, jnp.reshape(density, (1,)))


def solution(mesh):
    placed = (
        P(("chain", "slab"), None, None),
        P(("chain", "slab"), None, None),
        P(("chain", "slab"), None, None),
        P(),
        P(),
        P(),
    )
    return jax.shard_map(
        per_device,
        mesh=mesh,
        in_specs=placed,
        out_specs=(P(("chain", "slab"), None, None), P("chain")),
        check_vma=False,
    )
```

profile of v0, /device:TPU:16, one launch (start us, length us, event | category | flops | bytes accessed | tf_op | source)
XLA Modules:
  0.0 900.2 jit_solution(4330136956723541852)
XLA Ops:
  0.6 11.5 %copy.35 = s32[32,256,256]{2,0,1:T(8,128)} copy(s32[32,256,256]{2,1,0:T(8,128)} %param.8) | data formatting | bytes 16777216 | tf_op args[2]
  12.2 6.2 all-to-all-start.1
  18.4 11.6 %copy.32 = s32[32,256,256]{2,0,1:T(8,128)} copy(s32[32,256,256]{2,1,0:T(8,128)} %param.7) | data formatting | bytes 16777216 | tf_op args[1]
  30.0 170.9 %all-to-all-done.1 = s32[32,256,256]{2,0,1:T(8,128)} async-done(((s32[32,256,256]{2,0,1:T(8,128)}), s32[32,256,256]{2,0,1:T(8,128)}, u32[]{:S(2)}, u32[]{:S(2)}) %all-to-all-start.1) | async-done | bytes 8388640 | tf_op jit(solution)/shard_map/all_to_all | solution.py:47
  200.9 4.9 all-to-all-start
  205.9 10.7 %fusion.22 = f32[32,256,256]{1,2,0:T(8,128)S(1)} fusion(f32[32,256,256]{2,1,0:T(8,128)} %param.6, f32[256,256]{1,0:T(8,128)S(1)} %copy-done.2), kind=kOutput, calls=%fused_computation.24 | convolution fusion | flops 6442450944 | bytes 17039360 | tf_op jit(solution)/shard_map/abc,tc->abt/dot_general | solution.py:10
  216.6 8.9 convolution_bitcast_fusion
  225.5 10.3 %copy.39 = f32[32,256,256]{2,0,1:T(8,128)} copy(f32[32,256,256]{1,2,0:T(8,128)} %convolution_bitcast_fusion) | data formatting | bytes 16777216 | tf_op jit(solution)/shard_map/abc,yb->ayc/transpose | solution.py:14
  235.8 152.4 %all-to-all-done = s32[32,256,256]{2,0,1:T(8,128)} async-done(((s32[32,256,256]{2,0,1:T(8,128)}), s32[32,256,256]{2,0,1:T(8,128)}, u32[]{:S(2)}, u32[]{:S(2)}) %all-to-all-start) | async-done | bytes 8388640 | tf_op jit(solution)/shard_map/all_to_all | solution.py:46
  388.2 5.0 all-to-all-start.2
  393.2 8.2 copy_convert_fusion
  405.9 10.4 %copy.43 = f32[512,16,256]{0,2,1:T(8,128)} copy(f32[512,16,256]{2,1,0:T(8,128)} %bitcast.68) | data formatting | bytes 16777216 | tf_op jit(solution)/shard_map/convert_element_type | solution.py:51
  416.3 8.2 copy_convert_fusion.1
  428.9 10.1 %copy.44 = f32[512,16,256]{0,2,1:T(8,128)} copy(f32[512,16,256]{2,1,0:T(8,128)} %bitcast.70) | data formatting | bytes 16777216 | tf_op jit(solution)/shard_map/convert_element_type | solution.py:50
  439.0 136.6 %all-to-all-done.2 = f32[32,256,256]{2,0,1:T(8,128)} async-done(((f32[32,256,256]{2,0,1:T(8,128)}), f32[32,256,256]{2,0,1:T(8,128)}, u32[]{:S(2)}, u32[]{:S(2)}) %all-to-all-start.2) | async-done | bytes 8388640 | tf_op jit(solution)/shard_map/all_to_all | solution.py:34
  575.6 13.6 %copy.41 = f32[16,32,16,256]{3,2,1,0:T(8,128)} copy(f32[16,32,16,256]{3,1,2,0:T(8,128)} %bitcast.11) | data formatting | bytes 16777216 | tf_op jit(solution)/shard_map/all_to_all | solution.py:34
  589.2 37.1 %fusion.4 = (f32[]{:T(128)}, f32[16,256,512]{2,1,0:T(8,128)}) fusion(f32[512,16,256]{0,2,1:T(8,128)} %copy.44, f32[512,16,256]{0,2,1:T(8,128)} %copy.43, f32[512,512]{1,0:T(8,128)S(1)} %copy-done, f32[512,16,256]{2,1,0:T(8,128)} %bitcast.66), kind=kOutput, calls=%fused_computation.6 | convolution fusion | flops 12895387648 | bytes 34603012 | tf_op jit(solution)/shard_map/abc,xa->xbc/dot_general | solution.py:18
  626.3 20.3 %fusion.13 = f32[512,16,256]{0,2,1:T(8,128)} fusion(f32[512,16,256]{0,2,1:T(8,128)} %copy.44, f32[512,16,256]{0,2,1:T(8,128)S(1)} %bitcast.65, f32[16,256,512]{2,1,0:T(8,128)} %get-tuple-element.3, f32[512,512]{1,0:T(8,128)S(1)} %copy-done), kind=kOutput, calls=%fused_computation.17 | convolution fusion | flops 12891193344 | bytes 34603008 | tf_op jit(solution)/shard_map/xbc,xa->abc/dot_general | solution.py:30
  646.6 10.3 %copy.45 = f32[512,16,256]{2,1,0:T(8,128)} copy(f32[512,16,256]{0,2,1:T(8,128)} %fusion.13) | data formatting | bytes 16777216 | tf_op jit(solution)/shard_map/xbc,xa->abc/dot_general | solution.py:30
  656.8 4.6 all-to-all-start.3
  661.5 6.1 multiply_reduce_fusion
  668.9 193.6 %psum.7 = f32[]{:T(128)} all-reduce(f32[]{:T(128)S(6)} %add.5), channel_id=1, replica_groups=mesh['chain'=2,'slab'=16] {'slab'}, use_global_device_ids=true, to_apply=%region_2.0 | all-reduce | flops 1 | bytes 8 | tf_op jit(solution)/shard_map/psum | solution.py:58
  867.8 14.6 %fusion.18 = f32[32,256,256]{2,1,0:T(8,128)S(1)} fusion(f32[32,256,256]{2,1,0:T(8,128)S(1)} %bitcast.71, f32[256,256]{1,0:T(8,128)S(1)} %copy-done.1), kind=kOutput, calls=%fused_computation.20 | convolution fusion | flops 6442450944 | bytes 17039360 | tf_op jit(solution)/shard_map/ayc,yb->abc/dot_general | solution.py:26
  882.4 16.3 %multiply_subtract_fusion = f32[32,256,256]{2,1,0:T(8,128)} fusion(f32[32,256,256]{2,1,0:T(8,128)S(1)} %bitcast.63, f32[32,256,256]{2,1,0:T(8,128)S(1)} %fusion.18, f32[256,256]{1,0:T(8,128)S(1)} %copy-done.2), kind=kOutput, calls=%fused_computation.12 | convolution fusion | flops 6446645248 | bytes 25427968 | tf_op jit(solution)/shard_map/abt,tc->abc/dot_general | solution.py:22
  (20 shorter events, 13.4 us)
Async XLA Ops:
  0.6 588.6 %copy-start = (f32[512,512]{1,0:T(8,128)S(1)}, f32[512,512]{1,0:T(8,128)}, u32[]{:S(2)}) copy-start(f32[512,512]{1,0:T(8,128)} %param.9) | copy-start | bytes 3145732
  12.2 188.7 %all-to-all-start.1 = ((s32[32,256,256]{2,0,1:T(8,128)}), s32[32,256,256]{2,0,1:T(8,128)}, u32[]{:S(2)}, u32[]{:S(2)}) async-start(s32[32,256,256]{2,0,1:T(8,128)} %copy.35), calls=%async_computation.1 | async-start | bytes 16777216 | tf_op jit(solution)/shard_map/all_to_all | solution.py:47
  30.0 175.9 %copy-start.2 = (f32[256,256]{1,0:T(8,128)S(1)}, f32[256,256]{1,0:T(8,128)}, u32[]{:S(2)}) copy-start(f32[256,256]{1,0:T(8,128)} %param.11) | copy-start | bytes 786436
  200.9 187.3 %all-to-all-start = ((s32[32,256,256]{2,0,1:T(8,128)}), s32[32,256,256]{2,0,1:T(8,128)}, u32[]{:S(2)}, u32[]{:S(2)}) async-start(s32[32,256,256]{2,0,1:T(8,128)} %copy.32), calls=%async_computation | async-start | bytes 16777216 | tf_op jit(solution)/shard_map/all_to_all | solution.py:46
  205.9 10.7 %copy-start.1 = (f32[256,256]{1,0:T(8,128)S(1)}, f32[256,256]{1,0:T(8,128)}, u32[]{:S(2)}) copy-start(f32[256,256]{1,0:T(8,128)} %param.10) | copy-start | bytes 786436
  388.2 187.4 %all-to-all-start.2 = ((f32[32,256,256]{2,0,1:T(8,128)}), f32[32,256,256]{2,0,1:T(8,128)}, u32[]{:S(2)}, u32[]{:S(2)}) async-start(f32[32,256,256]{2,0,1:T(8,128)} %copy.39), calls=%async_computation.2 | async-start | bytes 16777216 | tf_op jit(solution)/shard_map/all_to_all | solution.py:34
  575.6 50.7 %slice-start.2 = ((s8[8388608]{0:T(1024)(128)(4,1)}), s8[4194304]{0:T(1024)(128)(4,1)S(1)}, s32[]{:S(2)}) async-start(s8[8388608]{0:T(1024)(128)(4,1)} %bitcast.64), calls=%async_computation.6 | async-start | bytes 8388608
  589.2 37.1 %slice-start.3 = ((s8[8388608]{0:T(1024)(128)(4,1)}), s8[4194304]{0:T(1024)(128)(4,1)S(1)}, s32[]{:S(2)}) async-start(s8[8388608]{0:T(1024)(128)(4,1)} %bitcast.64), calls=%async_computation.7 | async-start | bytes 8388608
  656.8 206.4 %all-to-all-start.3 = ((f32[512,16,256]{2,1,0:T(8,128)}), f32[512,16,256]{2,1,0:T(8,128)}, u32[]{:S(2)}, u32[]{:S(2)}) async-start(f32[512,16,256]{2,1,0:T(8,128)} %copy.45), calls=%async_computation.3 | async-start | bytes 16777216 | tf_op jit(solution)/shard_map/all_to_all | solution.py:38
  863.2 19.2 %slice-start = ((s8[8388608]{0:T(1024)(128)(4,1)}), s8[4194304]{0:T(1024)(128)(4,1)S(1)}, s32[]{:S(2)}) async-start(s8[8388608]{0:T(1024)(128)(4,1)} %bitcast.62), calls=%async_computation.4 | async-start | bytes 8388608
  867.8 14.6 %slice-start.1 = ((s8[8388608]{0:T(1024)(128)(4,1)}), s8[4194304]{0:T(1024)(128)(4,1)S(1)}, s32[]{:S(2)}) async-start(s8[8388608]{0:T(1024)(128)(4,1)} %bitcast.62), calls=%async_computation.5 | async-start | bytes 8388608
where the time goes:
time: 909 us; the launch traced here: 900 us
  waiting for transfers between devices  460 us (51%)
  blocking collectives  194 us (21%)
  matrix products  108 us (12%)
  local copies, waits for them, and re-layouts  91.2 us (10%)
  other arithmetic  22.6 us (2%)
  starting transfers between devices  20.8 us (2%)
    psum x1, blocking collectives, per_device(): total_sum = lax.psum(partial_sum, 'slab')  194 us
    all_to_all x1, waiting for transfers between devices, per_device(): lax.all_to_all(exposure, 'slab', split_axis=1, concat_axis=0, tiled=True)  171 us
    all_to_all x1, waiting for transfers between devices, per_device(): lax.all_to_all(counts, 'slab', split_axis=1, concat_axis=0, tiled=True)  152 us
    all_to_all x1, waiting for transfers between devices, to_lines(): lax.all_to_all(values, 'slab', split_axis=1, concat_axis=0, tiled=True)  137 us
    dot_general x1, matrix products, mode_first(): jnp.einsum('abc,xa->xbc', values, matrix, precision=lax.Precision.HIGHEST)  37.1 us
    unnamed x16, local copies, waits for them, and re-layouts  23.2 us
    dot_general x1, matrix products, adjoint_first(): jnp.einsum('xbc,xa->abc', values, matrix, precision=lax.Precision.HIGHEST)  20.3 us
  transfers between devices with their start and end apart: 4, of which 3 were waited for; matrix products, arithmetic and copies ran while one was open for 10% of the time, Pallas kernels for 0%

commit v1 on v0

--- a/solution.py
+++ b/solution.py
@@ -4,6 +4,12 @@
 from jax.sharding import PartitionSpec as P
 
 field_scale = 0.6
+
+
+def swap_blocks(value, name, split, join):
+    pieces = jnp.split(value, lax.axis_size(name), axis=split)
+    arrived = lax.all_to_all(jnp.stack(pieces), name, 0, 0)
+    return jnp.concatenate(arrived, axis=join)
 
 
 def mode_last(values, matrix):
@@ -44,7 +50,7 @@
     partly = mode_middle(mode_last(whitened, cholesky_time), cholesky_north)
     counts_lines, exposure_lines = (
         lax.all_to_all(counts, "slab", split_axis=1, concat_axis=0, tiled=True),
-        lax.all_to_all(exposure, "slab", split_axis=1, concat_axis=0, tiled=True),
+        swap_blocks(exposure, "slab", 1, 0),
     )
     log_lines = field_scale * mode_first(to_lines(partly), cholesky_east)
     observed = counts_lines.astype(jnp.float32)

time: 909 us -> 926 us (1.019)
  local copies, waits for them, and re-layouts: 91.2 us -> 105 us
    unnamed x16 -> x30, local copies, waits for them, and re-layouts: 23.2 us -> 40 us
where the time goes in v1:
time: 926 us; the launch traced here: 919 us
  waiting for transfers between devices  465 us (50%)
  blocking collectives  194 us (21%)
  matrix products  108 us (12%)
  local copies, waits for them, and re-layouts  105 us (11%)
  other arithmetic  22.3 us (2%)
  starting transfers between devices  20.9 us (2%)
    psum x1, blocking collectives, per_device(): total_sum = lax.psum(partial_sum, 'slab')  194 us
    all_to_all x1, waiting for transfers between devices, swap_blocks(): arrived = lax.all_to_all(jnp.stack(pieces), name, 0, 0)  171 us
    all_to_all x1, waiting for transfers between devices, per_device(): lax.all_to_all(counts, 'slab', split_axis=1, concat_axis=0, tiled=True)  152 us
    all_to_all x1, waiting for transfers between devices, to_lines(): lax.all_to_all(values, 'slab', split_axis=1, concat_axis=0, tiled=True)  142 us
    unnamed x30, local copies, waits for them, and re-layouts  40 us
    dot_general x1, matrix products, mode_first(): jnp.einsum('abc,xa->xbc', values, matrix, precision=lax.Precision.HIGHEST)  37.1 us
    dot_general x1, matrix products, adjoint_first(): jnp.einsum('xbc,xa->abc', values, matrix, precision=lax.Precision.HIGHEST)  20.3 us
  transfers between devices with their start and end apart: 4, of which 3 were waited for; matrix products, arithmetic and copies ran while one was open for 10% of the time, Pallas kernels for 0%

profile of v1, /device:TPU:16, one launch (start us, length us, event | category | flops | bytes accessed | tf_op | source)
XLA Modules:
  0.0 918.9 jit_solution(11005668251070183937)
XLA Ops:
  30.9 6.2 all-to-all-start.1
  37.0 11.6 %copy.31 = s32[32,256,256]{2,0,1:T(8,128)} copy(s32[32,256,256]{2,1,0:T(8,128)} %param.7) | data formatting | bytes 16777216 | tf_op args[1]
  48.7 170.9 %all-to-all-done.1 = s32[16,32,16,256]{3,2,1,0:T(8,128)} async-done(((s32[16,32,16,256]{3,2,1,0:T(8,128)}), s32[16,32,16,256]{3,2,1,0:T(8,128)}, u32[]{:S(2)}, u32[]{:S(2)}) %all-to-all-start.1) | async-done | bytes 8388640 | tf_op jit(solution)/shard_map/all_to_all | solution.py:11
  219.6 5.2 all-to-all-start
  224.8 10.7 %fusion.22 = f32[32,256,256]{1,2,0:T(8,128)S(1)} fusion(f32[32,256,256]{2,1,0:T(8,128)} %param.6, f32[256,256]{1,0:T(8,128)S(1)} %copy-done.2), kind=kOutput, calls=%fused_computation.39 | convolution fusion | flops 6442450944 | bytes 17039360 | tf_op jit(solution)/shard_map/abc,tc->abt/dot_general | solution.py:16
  235.5 8.9 convolution_bitcast_fusion
  244.4 10.3 %copy.35 = f32[32,256,256]{2,0,1:T(8,128)} copy(f32[32,256,256]{1,2,0:T(8,128)} %convolution_bitcast_fusion) | data formatting | bytes 16777216 | tf_op jit(solution)/shard_map/abc,yb->ayc/transpose | solution.py:20
  254.7 152.4 %all-to-all-done = s32[32,256,256]{2,0,1:T(8,128)} async-done(((s32[32,256,256]{2,0,1:T(8,128)}), s32[32,256,256]{2,0,1:T(8,128)}, u32[]{:S(2)}, u32[]{:S(2)}) %all-to-all-start) | async-done | bytes 8388640 | tf_op jit(solution)/shard_map/all_to_all | solution.py:52
  407.2 4.9 all-to-all-start.2
  412.1 7.9 convert_element_type.22
  420.0 10.0 %copy.39 = f32[512,16,256]{0,2,1:T(8,128)} copy(f32[512,16,256]{2,1,0:T(8,128)} %bitcast.96) | data formatting | bytes 16777216 | tf_op jit(solution)/shard_map/convert_element_type | solution.py:57
  430.0 8.2 copy_convert_fusion
  442.6 10.0 %copy.40 = f32[512,16,256]{0,2,1:T(8,128)} copy(f32[512,16,256]{2,1,0:T(8,128)} %bitcast.98) | data formatting | bytes 16777216 | tf_op jit(solution)/shard_map/convert_element_type | solution.py:56
  452.6 141.9 %all-to-all-done.2 = f32[32,256,256]{2,0,1:T(8,128)} async-done(((f32[32,256,256]{2,0,1:T(8,128)}), f32[32,256,256]{2,0,1:T(8,128)}, u32[]{:S(2)}, u32[]{:S(2)}) %all-to-all-start.2) | async-done | bytes 8388640 | tf_op jit(solution)/shard_map/all_to_all | solution.py:40
  594.5 13.6 %copy.37 = f32[16,32,16,256]{3,2,1,0:T(8,128)} copy(f32[16,32,16,256]{3,1,2,0:T(8,128)} %bitcast.25) | data formatting | bytes 16777216 | tf_op jit(solution)/shard_map/all_to_all | solution.py:40
  608.1 37.1 %fusion.4 = (f32[]{:T(128)}, f32[16,256,512]{2,1,0:T(8,128)}) fusion(f32[512,16,256]{0,2,1:T(8,128)} %copy.40, f32[512,16,256]{0,2,1:T(8,128)} %copy.39, f32[512,512]{1,0:T(8,128)S(1)} %copy-done, f32[512,16,256]{2,1,0:T(8,128)} %bitcast.95), kind=kOutput, calls=%fused_computation.6 | convolution fusion | flops 12895387648 | bytes 34603012 | tf_op jit(solution)/shard_map/abc,xa->xbc/dot_general | solution.py:24
  645.2 20.3 %fusion.13 = f32[512,16,256]{0,2,1:T(8,128)} fusion(f32[512,16,256]{0,2,1:T(8,128)} %copy.40, f32[512,16,256]{0,2,1:T(8,128)S(1)} %bitcast.94, f32[16,256,512]{2,1,0:T(8,128)} %get-tuple-element.3, f32[512,512]{1,0:T(8,128)S(1)} %copy-done), kind=kOutput, calls=%fused_computation.16 | convolution fusion | flops 12891193344 | bytes 34603008 | tf_op jit(solution)/shard_map/xbc,xa->abc/dot_general | solution.py:36
  665.4 10.3 %copy.41 = f32[512,16,256]{2,1,0:T(8,128)} copy(f32[512,16,256]{0,2,1:T(8,128)} %fusion.13) | data formatting | bytes 16777216 | tf_op jit(solution)/shard_map/xbc,xa->abc/dot_general | solution.py:36
  675.7 4.6 all-to-all-start.3
  680.3 6.1 multiply_reduce_fusion
  687.8 193.6 %psum.7 = f32[]{:T(128)} all-reduce(f32[]{:T(128)S(6)} %add.5), channel_id=1, replica_groups=mesh['chain'=2,'slab'=16] {'slab'}, use_global_device_ids=true, to_apply=%region_2.0 | all-reduce | flops 1 | bytes 8 | tf_op jit(solution)/shard_map/psum | solution.py:64
  882.1 4.6 copy.42
  886.7 14.6 %fusion.18 = f32[32,256,256]{2,1,0:T(8,128)S(1)} fusion(f32[32,256,256]{2,1,0:T(8,128)S(1)} %bitcast.99, f32[256,256]{1,0:T(8,128)S(1)} %copy-done.1), kind=kOutput, calls=%fused_computation.35 | convolution fusion | flops 6442450944 | bytes 17039360 | tf_op jit(solution)/shard_map/ayc,yb->abc/dot_general | solution.py:32
  901.3 16.3 %multiply_subtract_fusion = f32[32,256,256]{2,1,0:T(8,128)} fusion(f32[32,256,256]{2,1,0:T(8,128)S(1)} %bitcast.92, f32[32,256,256]{2,1,0:T(8,128)S(1)} %fusion.18, f32[256,256]{1,0:T(8,128)S(1)} %copy-done.2), kind=kOutput, calls=%fused_computation.11 | convolution fusion | flops 6446645248 | bytes 25427968 | tf_op jit(solution)/shard_map/abt,tc->abc/dot_general | solution.py:28
  (34 shorter events, 34.6 us)
Async XLA Ops:
  0.6 607.4 %copy-start = (f32[512,512]{1,0:T(8,128)S(1)}, f32[512,512]{1,0:T(8,128)}, u32[]{:S(2)}) copy-start(f32[512,512]{1,0:T(8,128)} %param.9) | copy-start | bytes 3145732
  30.9 188.7 %all-to-all-start.1 = ((s32[16,32,16,256]{3,2,1,0:T(8,128)}), s32[16,32,16,256]{3,2,1,0:T(8,128)}, u32[]{:S(2)}, u32[]{:S(2)}) async-start(s32[16,32,16,256]{3,2,1,0:T(8,128)} %bitcast_dynamic-update-slice_fusion), calls=%async_computation.1 | async-start | bytes 16777216 | tf_op jit(solution)/shard_map/all_to_all | solution.py:11
  48.7 176.1 %copy-start.2 = (f32[256,256]{1,0:T(8,128)S(1)}, f32[256,256]{1,0:T(8,128)}, u32[]{:S(2)}) copy-start(f32[256,256]{1,0:T(8,128)} %param.11) | copy-start | bytes 786436
  219.6 187.6 %all-to-all-start = ((s32[32,256,256]{2,0,1:T(8,128)}), s32[32,256,256]{2,0,1:T(8,128)}, u32[]{:S(2)}, u32[]{:S(2)}) async-start(s32[32,256,256]{2,0,1:T(8,128)} %copy.31), calls=%async_computation | async-start | bytes 16777216 | tf_op jit(solution)/shard_map/all_to_all | solution.py:52
  224.8 10.7 %copy-start.1 = (f32[256,256]{1,0:T(8,128)S(1)}, f32[256,256]{1,0:T(8,128)}, u32[]{:S(2)}) copy-start(f32[256,256]{1,0:T(8,128)} %param.10) | copy-start | bytes 786436
  407.2 187.3 %all-to-all-start.2 = ((f32[32,256,256]{2,0,1:T(8,128)}), f32[32,256,256]{2,0,1:T(8,128)}, u32[]{:S(2)}, u32[]{:S(2)}) async-start(f32[32,256,256]{2,0,1:T(8,128)} %copy.35), calls=%async_computation.2 | async-start | bytes 16777216 | tf_op jit(solution)/shard_map/all_to_all | solution.py:40
  594.5 50.7 %slice-start.2 = ((s8[8388608]{0:T(1024)(128)(4,1)}), s8[4194304]{0:T(1024)(128)(4,1)S(1)}, s32[]{:S(2)}) async-start(s8[8388608]{0:T(1024)(128)(4,1)} %bitcast.93), calls=%async_computation.6 | async-start | bytes 8388608
  608.1 37.1 %slice-start.3 = ((s8[8388608]{0:T(1024)(128)(4,1)}), s8[4194304]{0:T(1024)(128)(4,1)S(1)}, s32[]{:S(2)}) async-start(s8[8388608]{0:T(1024)(128)(4,1)} %bitcast.93), calls=%async_computation.7 | async-start | bytes 8388608
  675.7 206.4 %all-to-all-start.3 = ((f32[512,16,256]{2,1,0:T(8,128)}), f32[512,16,256]{2,1,0:T(8,128)}, u32[]{:S(2)}, u32[]{:S(2)}) async-start(f32[512,16,256]{2,1,0:T(8,128)} %copy.41), calls=%async_computation.3 | async-start | bytes 16777216 | tf_op jit(solution)/shard_map/all_to_all | solution.py:44
  882.1 19.2 %slice-start = ((s8[8388608]{0:T(1024)(128)(4,1)}), s8[4194304]{0:T(1024)(128)(4,1)S(1)}, s32[]{:S(2)}) async-start(s8[8388608]{0:T(1024)(128)(4,1)} %bitcast.91), calls=%async_computation.4 | async-start | bytes 8388608
  886.7 14.6 %slice-start.1 = ((s8[8388608]{0:T(1024)(128)(4,1)}), s8[4194304]{0:T(1024)(128)(4,1)S(1)}, s32[]{:S(2)}) async-start(s8[8388608]{0:T(1024)(128)(4,1)} %bitcast.91), calls=%async_computation.5 | async-start | bytes 8388608
